TPU v7x, 32 devices: a whole 2x2x4 slice. The times are simulated.
32 devices in a mesh: mem: 8 (over y, x, core), st: 4 (over z).
Axes of the slice: x: 2, y: 2, z: 4, core: 2. Of those that a mesh axis runs over, the one named last changes fastest.
Arguments:
- ensemble: float32 [8192, 256], P('st', 'mem'), may hold values from -8 to 8
- obs_values: float32 [4, 8, 128], replicated, may hold values from -8 to 8
- obs_sigma: float32 [4, 8, 128], replicated, may hold values from 0.25 to 0.5
- obs_operator: float32 [4, 8, 2, 128, 128], replicated, may hold values from -0.375 to 0.375
- block_cols: int32 [4, 8, 2], replicated, may hold values from 0 to 63
- batch_order: int32 [4], replicated, may hold values from 0 to 3, each once
Outputs:
- analysis: float32 [8192, 256], P('st', 'mem')
- log_weights: float32 [256], P('mem')
- ess: float32 [], replicated
Inputs may be any that keep to these rules, and one draw needn't show every extreme that they name: `block_cols`: block indices of the whole state. `batch_order`: each batch exactly once.
All inputs are finite; a program needn't handle non-finite values.
Results may differ from a plain program's by a relative error of at most 0.0003.
Values sent between devices are 32-bit elements; how exact they have to be, the bound alone decides.
A program may use at most 64 MiB of HBM per device.

v0:
```python
import math
import jax
import jax.numpy as jnp
from jax import lax
from jax.sharding import PartitionSpec as P

precise = lax.Precision.HIGHEST


def solve_blocks(moment, target):
    factor = jnp.linalg.cholesky(moment)
    return jax.vmap(lambda lower, right: jax.scipy.linalg.cho_solve((lower, True), right))(
        factor, target
    )


def shards(ensemble, obs_values, obs_sigma, obs_operator, block_cols, batch_order):
    block_size = obs_operator.shape[-1]
    row_count, mem_dev = ensemble.shape
    nblocks = row_count // block_size
    members = mem_dev * lax.axis_size("mem")
    batches, obs_blocks, col_count = block_cols.shape
    temper = 1.0 / math.sqrt(batches * obs_blocks * block_size)
    offset = lax.axis_index("st") * nblocks
    states = ensemble.reshape(nblocks, block_size, mem_dev)
    eye = jnp.eye(block_size, dtype=jnp.float32)
    slots = jnp.arange(nblocks, dtype=jnp.int32)
    loglik = jnp.zeros((mem_dev,), jnp.float32)
    for batch_step in range(batches):
        chosen = batch_order[batch_step]
        operator_now = lax.dynamic_index_in_dim(obs_operator, chosen, 0, keepdims=False)
        columns = lax.dynamic_index_in_dim(block_cols, chosen, 0, keepdims=False)
        values_now = lax.dynamic_index_in_dim(obs_values, chosen, 0, keepdims=False)
        sigma_now = lax.dynamic_index_in_dim(obs_sigma, chosen, 0, keepdims=False)
        local_ids = columns.reshape(-1) - offset
        selector = (local_ids[:, None] == slots[None, :]).astype(jnp.float32)
        picked = jnp.einsum("ps,sim->pim", selector, states, precision=precise)
        picked = picked.reshape(obs_blocks, col_count, block_size, mem_dev)
        partial_value = jnp.einsum("bkij,bkjm->bim", operator_now, picked, precision=precise)
        image = lax.psum(partial_value, "st")
        misfit = (values_now[:, :, None] - image) / sigma_now[:, :, None]
        loglik = loglik - 0.5 * temper * jnp.sum(misfit * misfit, axis=(0, 1))
        center = lax.psum(jnp.sum(image, axis=2), "mem") / members
        anomaly = image - center[:, :, None]
        moment_sum, cross_sum = lax.psum(
            (
                jnp.einsum("bim,bjm->bij", anomaly, anomaly, precision=precise),
                jnp.einsum("bkim,bjm->bkij", picked, anomaly, precision=precise),
            ),
            "mem",
        )
        moment = moment_sum / (members - 1) + eye * (sigma_now * sigma_now)[:, :, None]
        cross = cross_sum / (members - 1)
        target = (values_now - center)[:, :, None] - 0.5 * anomaly
        weights = solve_blocks(moment, target)
        change = jnp.einsum("bkij,bjm->bkim", cross, weights, precision=precise)
        change = change.reshape(obs_blocks * col_count, block_size, mem_dev)
        states = states + jnp.einsum("ps,pim->sim", selector, change, precision=precise)
    largest_local = jnp.max(loglik)
    largest = lax.pmax(largest_local, "mem")
    scaled = jnp.exp(loglik - largest)
    summed, squares = lax.psum((jnp.sum(scaled), jnp.sum(scaled * scaled)), "mem")
    log_weights = loglik - largest - jnp.log(summed)
    ess = summed * summed / squares
    return (states.reshape(row_count, mem_dev), log_weights, ess)


def solution(mesh):
    placed = (P("st", "mem"), P(), P(), P(), P(), P())
    return jax.shard_map(
        shards,
        mesh=mesh,
        in_specs=placed,
        out_specs=(P("st", "mem"), P("mem"), P()),
        check_vma=False,
    )
```

profile of v0, /device:TPU:0, one launch (start us, length us, event | category | flops | bytes accessed | tf_op | source)
XLA Modules:
  0.0 1220.0 jit_solution(10032874839914542183)
XLA Ops:
  23.3 35.7 %all-reduce.14.cloned.1.call-done = f32[8,128,32]{1,2,0:T(8,128)} async-done(((f32[8,128,32]{1,2,0:T(8,128)}), f32[8,128,32]{1,2,0:T(8,128)}) %all-reduce.14.cloned.1.call-update) | async-done | bytes 131088 | tf_op jit(solution)/shard_map/psum | solution.py:40
  60.1 11.8 psum.127
  71.9 3.9 fusion.50
  79.3 57.4 %all-reduce.28.cloned.1.call-done = (f32[8,128,128]{1,2,0:T(8,128)}, f32[8,2,128,128]{3,2,1,0:T(8,128)}) async-done(((f32[8,128,128]{1,2,0:T(8,128)}, f32[8,2,128,128]{3,2,1,0:T(8,128)}), (f32[8,128,128]{1,2,0:T(8,128)}, f32[8,2,128,128]{3,2,1,0:T(8,128)})) %all-reduce.28.cloned.1.call-update) | async-done | bytes 1572880 | tf_op jit(solution)/shard_map/psum | solution.py:45
  139.2 93.8 %custom-call.14 = f32[8,128,128]{2,1,0:T(8,128)S(1)} custom-call(f32[8,128,128]{2,1,0:T(8,128)S(1)} %fusion.31), custom_call_target="Cholesky" | custom-call | tf_op jit(solution)/shard_map/jit(cholesky)/cholesky | solution.py:11
  233.3 78.6 %custom-call.15 = f32[8,1,128,128]{2,3,1,0:T(8,128)S(1)} custom-call(f32[8,1,128,128]{3,2,1,0:T(8,128)S(1)} %select_bitcast_fusion.3), custom_call_target="InvertDiagBlocksLowerTriangular" | custom-call | tf_op jit(solution)/shard_map/vmap(jit(_cho_solve))/triangular_solve | solution.py:12
  318.5 33.9 %all-reduce.16.cloned.1.call-done = f32[8,128,32]{1,2,0:T(8,128)} async-done(((f32[8,128,32]{1,2,0:T(8,128)}), f32[8,128,32]{1,2,0:T(8,128)}) %all-reduce.16.cloned.1.call-update) | async-done | bytes 131088 | tf_op jit(solution)/shard_map/psum | solution.py:40
  353.4 12.0 psum.131
  365.4 3.9 fusion.47
  372.4 57.8 %all-reduce.26.cloned.1.call-done = (f32[8,128,128]{1,2,0:T(8,128)}, f32[8,2,128,128]{3,2,1,0:T(8,128)}) async-done(((f32[8,128,128]{1,2,0:T(8,128)}, f32[8,2,128,128]{3,2,1,0:T(8,128)}), (f32[8,128,128]{1,2,0:T(8,128)}, f32[8,2,128,128]{3,2,1,0:T(8,128)})) %all-reduce.26.cloned.1.call-update) | async-done | bytes 1572880 | tf_op jit(solution)/shard_map/psum | solution.py:45
  432.8 93.8 %custom-call.16 = f32[8,128,128]{2,1,0:T(8,128)S(1)} custom-call(f32[8,128,128]{2,1,0:T(8,128)S(1)} %fusion.27), custom_call_target="Cholesky" | custom-call | tf_op jit(solution)/shard_map/jit(cholesky)/cholesky | solution.py:11
  526.9 78.6 %custom-call.17 = f32[8,1,128,128]{2,3,1,0:T(8,128)S(1)} custom-call(f32[8,1,128,128]{3,2,1,0:T(8,128)S(1)} %select_bitcast_fusion.2), custom_call_target="InvertDiagBlocksLowerTriangular" | custom-call | tf_op jit(solution)/shard_map/vmap(jit(_cho_solve))/triangular_solve | solution.py:12
  612.0 33.9 %all-reduce.18.cloned.1.call-done = f32[8,128,32]{1,2,0:T(8,128)} async-done(((f32[8,128,32]{1,2,0:T(8,128)}), f32[8,128,32]{1,2,0:T(8,128)}) %all-reduce.18.cloned.1.call-update) | async-done | bytes 131088 | tf_op jit(solution)/shard_map/psum | solution.py:40
  647.0 12.2 %psum.135 = f32[8,128]{1,0:T(8,128)S(1)} all-reduce(f32[8,128]{1,0:T(8,128)S(1)} %get-tuple-element.10), channel_id=1, replica_groups=mesh['mem'=8,'st'=4] {'mem'}, use_global_device_ids=true, to_apply=%region_14.17 | all-reduce | flops 1024 | bytes 8192 | tf_op jit(solution)/shard_map/psum | solution.py:43
  666.2 57.8 %all-reduce.24.cloned.1.call-done = (f32[8,128,128]{1,2,0:T(8,128)}, f32[8,2,128,128]{3,2,1,0:T(8,128)}) async-done(((f32[8,128,128]{1,2,0:T(8,128)}, f32[8,2,128,128]{3,2,1,0:T(8,128)}), (f32[8,128,128]{1,2,0:T(8,128)}, f32[8,2,128,128]{3,2,1,0:T(8,128)})) %all-reduce.24.cloned.1.call-update) | async-done | bytes 1572880 | tf_op jit(solution)/shard_map/psum | solution.py:45
  726.5 93.8 %custom-call.18 = f32[8,128,128]{2,1,0:T(8,128)S(1)} custom-call(f32[8,128,128]{2,1,0:T(8,128)S(1)} %fusion.23), custom_call_target="Cholesky" | custom-call | tf_op jit(solution)/shard_map/jit(cholesky)/cholesky | solution.py:11
  820.6 78.6 %custom-call.19 = f32[8,1,128,128]{2,3,1,0:T(8,128)S(1)} custom-call(f32[8,1,128,128]{3,2,1,0:T(8,128)S(1)} %select_bitcast_fusion.1), custom_call_target="InvertDiagBlocksLowerTriangular" | custom-call | tf_op jit(solution)/shard_map/vmap(jit(_cho_solve))/triangular_solve | solution.py:12
  905.8 33.9 %all-reduce.20.cloned.1.call-done = f32[8,128,32]{1,2,0:T(8,128)} async-done(((f32[8,128,32]{1,2,0:T(8,128)}), f32[8,128,32]{1,2,0:T(8,128)}) %all-reduce.20.cloned.1.call-update) | async-done | bytes 131088 | tf_op jit(solution)/shard_map/psum | solution.py:40
  941.3 12.4 %pmax.7 = f32[]{:T(128)} all-reduce(f32[]{:T(128)} %get-tuple-element.28), channel_id=1, replica_groups=mesh['mem'=8,'st'=4] {'mem'}, use_global_device_ids=true, to_apply=%region_27.30 | all-reduce | flops 1 | bytes 8 | tf_op jit(solution)/shard_map/pmax | solution.py:60
  955.0 12.8 %all-reduce = (f32[8,128]{1,0:T(8,128)S(1)}, f32[]{:T(128)}, f32[]{:T(128)}) all-reduce(f32[8,128]{1,0:T(8,128)S(1)} %get-tuple-element.12, f32[]{:T(128)} %get-tuple-element.14, f32[]{:T(128)} %get-tuple-element.13), channel_id=1, replica_groups=mesh['mem'=8,'st'=4] {'mem'}, use_global_device_ids=true, to_apply=%region_19.22 | all-reduce | flops 1026 | bytes 8208 | tf_op jit(solution)/shard_map/psum | solution.py:43
  967.8 3.9 fusion.41
  978.4 54.3 %all-reduce.22.cloned.1.call-done = (f32[8,128,128]{1,2,0:T(8,128)}, f32[8,2,128,128]{3,2,1,0:T(8,128)}) async-done(((f32[8,128,128]{1,2,0:T(8,128)}, f32[8,2,128,128]{3,2,1,0:T(8,128)}), (f32[8,128,128]{1,2,0:T(8,128)}, f32[8,2,128,128]{3,2,1,0:T(8,128)})) %all-reduce.22.cloned.1.call-update) | async-done | bytes 1572880 | tf_op jit(solution)/shard_map/psum | solution.py:45
  1035.2 93.8 %custom-call.20 = f32[8,128,128]{2,1,0:T(8,128)S(1)} custom-call(f32[8,128,128]{2,1,0:T(8,128)S(1)} %fusion.19), custom_call_target="Cholesky" | custom-call | tf_op jit(solution)/shard_map/jit(cholesky)/cholesky | solution.py:11
  1129.3 78.6 %custom-call.21 = f32[8,1,128,128]{2,3,1,0:T(8,128)S(1)} custom-call(f32[8,1,128,128]{3,2,1,0:T(8,128)S(1)} %select_bitcast_fusion), custom_call_target="InvertDiagBlocksLowerTriangular" | custom-call | tf_op jit(solution)/shard_map/vmap(jit(_cho_solve))/triangular_solve | solution.py:12
  (113 shorter events, 66.5 us)
Async XLA Ops:
  7.2 51.9 %all-reduce.14.cloned.1.call-start = ((), (), s32[]{:S(2)}) async-start(), calls=%async_computation | async-start | bytes 262144 | tf_op jit(solution)/shard_map/psum | solution.py:40
  21.8 114.9 %all-reduce.28.cloned.1.call-start = ((), (), s32[]{:S(2)}) async-start(), calls=%async_computation.7 | async-start | bytes 3145728 | tf_op jit(solution)/shard_map/psum | solution.py:45
  75.8 236.1 %copy-start.1 = (f32[8,128,32]{1,2,0:T(8,128)S(1)}, f32[8,128,32]{1,2,0:T(8,128)}, u32[]{:S(2)}) copy-start(f32[8,128,32]{1,2,0:T(8,128)} %all-reduce.14.cloned.1.call-done) | copy-start | bytes 393220
  78.7 273.7 %all-reduce.16.cloned.1.call-start = ((), (), s32[]{:S(2)}) async-start(), calls=%async_computation.1 | async-start | bytes 262144 | tf_op jit(solution)/shard_map/psum | solution.py:40
  136.7 176.7 %copy-start.5 = (f32[8,2,128,128]{3,2,1,0:T(8,128)S(1)}, f32[8,2,128,128]{3,2,1,0:T(8,128)}, u32[]{:S(2)}) copy-start(f32[8,2,128,128]{3,2,1,0:T(8,128)} %get-tuple-element.25) | copy-start | bytes 3145732
  318.5 111.8 %all-reduce.26.cloned.1.call-start = ((), (), s32[]{:S(2)}) async-start(), calls=%async_computation.6 | async-start | bytes 3145728 | tf_op jit(solution)/shard_map/psum | solution.py:45
  369.3 236.1 %copy-start.3 = (f32[8,128,32]{1,2,0:T(8,128)S(1)}, f32[8,128,32]{1,2,0:T(8,128)}, u32[]{:S(2)}) copy-start(f32[8,128,32]{1,2,0:T(8,128)} %all-reduce.16.cloned.1.call-done) | copy-start | bytes 393220
  372.2 273.7 %all-reduce.18.cloned.1.call-start = ((), (), s32[]{:S(2)}) async-start(), calls=%async_computation.2 | async-start | bytes 262144 | tf_op jit(solution)/shard_map/psum | solution.py:40
  430.2 176.7 %copy-start.7 = (f32[8,2,128,128]{3,2,1,0:T(8,128)S(1)}, f32[8,2,128,128]{3,2,1,0:T(8,128)}, u32[]{:S(2)}) copy-start(f32[8,2,128,128]{3,2,1,0:T(8,128)} %get-tuple-element.23) | copy-start | bytes 3145732
  612.0 112.0 %all-reduce.24.cloned.1.call-start = ((), (), s32[]{:S(2)}) async-start(), calls=%async_computation.5 | async-start | bytes 3145728 | tf_op jit(solution)/shard_map/psum | solution.py:45
  663.1 236.1 %copy-start.2 = (f32[8,128,32]{1,2,0:T(8,128)S(1)}, f32[8,128,32]{1,2,0:T(8,128)}, u32[]{:S(2)}) copy-start(f32[8,128,32]{1,2,0:T(8,128)} %all-reduce.18.cloned.1.call-done) | copy-start | bytes 393220
  666.0 273.7 %all-reduce.20.cloned.1.call-start = ((), (), s32[]{:S(2)}) async-start(), calls=%async_computation.3 | async-start | bytes 262144 | tf_op jit(solution)/shard_map/psum | solution.py:40
  724.0 176.7 %copy-start.6 = (f32[8,2,128,128]{3,2,1,0:T(8,128)S(1)}, f32[8,2,128,128]{3,2,1,0:T(8,128)}, u32[]{:S(2)}) copy-start(f32[8,2,128,128]{3,2,1,0:T(8,128)} %get-tuple-element.21) | copy-start | bytes 3145732
  905.7 127.0 %all-reduce.22.cloned.1.call-start = ((), (), s32[]{:S(2)}) async-start(), calls=%async_computation.4 | async-start | bytes 3145728 | tf_op jit(solution)/shard_map/psum | solution.py:45
  971.7 236.2 %copy-start = (f32[8,128,32]{1,2,0:T(8,128)S(1)}, f32[8,128,32]{1,2,0:T(8,128)}, u32[]{:S(2)}) copy-start(f32[8,128,32]{1,2,0:T(8,128)} %all-reduce.20.cloned.1.call-done) | copy-start | bytes 393220
  1032.7 176.7 %copy-start.4 = (f32[8,2,128,128]{3,2,1,0:T(8,128)S(1)}, f32[8,2,128,128]{3,2,1,0:T(8,128)}, u32[]{:S(2)}) copy-start(f32[8,2,128,128]{3,2,1,0:T(8,128)} %get-tuple-element.19) | copy-start | bytes 3145732
Sparse Core Ops, SparseCore 0:
  21.9 37.1 all-reduce.13
  78.8 57.8 all-reduce.27
  318.6 33.7 all-reduce.15
  372.3 57.8 all-reduce.25
  612.1 33.7 all-reduce.17
  666.1 57.8 all-reduce.23
  905.9 33.7 all-reduce.19
  974.7 57.9 all-reduce.21
where the time goes:
time: 1220 us
  other arithmetic  709 us (58%)
  waiting for transfers between devices  365 us (30%)
  blocking collectives  61.3 us (5%)
  matrix products  52.9 us (4%)
  between operations  26.4 us (2%)
    another operation x13, other arithmetic, solve_blocks(): factor = jnp.linalg.cholesky(moment)  376 us
    another operation x9, other arithmetic, solve_blocks(): jax.scipy.linalg.cho_solve((lower, True), right)  315 us
    psum x4, waiting for transfers between devices, shards(): lax.psum((jnp.einsum('bim,bjm->bij', anomaly, anomaly, precision=precise)...  227 us
    psum x4, waiting for transfers between devices, shards(): image = lax.psum(partial_value, 'st')  137 us
    psum x4, blocking collectives, shards(): center = lax.psum(jnp.sum(image, axis=2), 'mem') / members  48.9 us
  transfers between devices with their start and end apart: 8, of which 8 were waited for; matrix products, arithmetic and copies ran while one was open for 0% of the time, Pallas kernels for 0%

commit v1 on v0

--- a/solution.py
+++ b/solution.py
@@ -1,3 +1,4 @@
+import functools
 import math
 import jax
 import jax.numpy as jnp
@@ -5,6 +6,13 @@
 from jax.sharding import PartitionSpec as P
 
 precise = lax.Precision.HIGHEST
+
+
+def store_the_digits(obj, axis_name):
+    return jnp.sum(lax.all_gather(obj, axis_name), axis=0)
+
+
+core_set = functools.partial(store_the_digits, axis_name="st")
 
 
 def solve_blocks(moment, target):
@@ -37,7 +45,7 @@
         picked = jnp.einsum("ps,sim->pim", selector, states, precision=precise)
         picked = picked.reshape(obs_blocks, col_count, block_size, mem_dev)
         partial_value = jnp.einsum("bkij,bkjm->bim", operator_now, picked, precision=precise)
-        image = lax.psum(partial_value, "st")
+        image = core_set(partial_value)
         misfit = (values_now[:, :, None] - image) / sigma_now[:, :, None]
         loglik = loglik - 0.5 * temper * jnp.sum(misfit * misfit, axis=(0, 1))
         center = lax.psum(jnp.sum(image, axis=2), "mem") / members

time: 1220 us -> 1140 us (0.934)
  waiting for transfers between devices: 365 us -> 231 us
  blocking collectives: 61.3 us -> 124 us
    psum x4 -> x0, waiting for transfers between devices: 137 us -> none  [shards(): image = lax.psum(partial_value, 'st')]
    all_gather x0 -> x4, blocking collectives: none -> 62.6 us  [store_the_digits(): return jnp.sum(lax.all_gather(obj, axis_name), axis=0)]
  transfers between devices with their start and end apart: 8 -> 4, of which waited for: 8 -> 4; matrix products, arithmetic and copies ran while one was open for 0% -> 0% of each run, Pallas kernels for 0% -> 0%
where the time goes in v1:
time: 1140 us; the launch traced here: 1130 us
  other arithmetic  705 us (62%)
  waiting for transfers between devices  231 us (20%)
  blocking collectives  124 us (11%)
  matrix products  42.4 us (4%)
  between operations  26.1 us (2%)
    another operation x13, other arithmetic, solve_blocks(): factor = jnp.linalg.cholesky(moment)  376 us
    another operation x9, other arithmetic, solve_blocks(): jax.scipy.linalg.cho_solve((lower, True), right)  315 us
    psum x4, waiting for transfers between devices, shards(): lax.psum((jnp.einsum('bim,bjm->bij', anomaly, anomaly, precision=precise)...  231 us
    all_gather x4, blocking collectives, store_the_digits(): return jnp.sum(lax.all_gather(obj, axis_name), axis=0)  62.6 us
    psum x4, blocking collectives, shards(): center = lax.psum(jnp.sum(image, axis=2), 'mem') / members  49.3 us
  transfers between devices with their start and end apart: 4, of which 4 were waited for; matrix products, arithmetic and copies ran while one was open for 0% of the time, Pallas kernels for 0%

profile of v1, /device:TPU:0, one launch (start us, length us, event | category | flops | bytes accessed | tf_op | source)
XLA Modules:
  0.0 1134.0 jit_solution(12855763376074155377)
XLA Ops:
  21.1 17.4 %all-gather = f32[32,128,32]{1,2,0:T(8,128)S(1)} all-gather(f32[8,128,32]{1,2,0:T(8,128)S(1)} %convolution_bitcast_fusion.7), channel_id=2, replica_groups=mesh['mem'=8,'st'=4] {'st'}, dimensions={0}, use_global_device_ids=true | all-gather | bytes 655360 | tf_op jit(solution)/shard_map/all_gather | solution.py:12
  38.6 12.2 %psum.98 = f32[8,128]{1,0:T(8,128)S(1)} all-reduce(f32[8,128]{1,0:T(8,128)S(1)} %bitcast_reduce_fusion.3), channel_id=1, replica_groups=mesh['mem'=8,'st'=4] {'mem'}, use_global_device_ids=true, to_apply=%region_2.3 | all-reduce | flops 1024 | bytes 8192 | tf_op jit(solution)/shard_map/psum | solution.py:51
  52.6 3.0 fusion.50
  56.3 59.0 %all-reduce.16.cloned.1.call-done = (f32[8,128,128]{1,2,0:T(8,128)}, f32[8,2,128,128]{3,2,1,0:T(8,128)}) async-done(((f32[8,128,128]{1,2,0:T(8,128)}, f32[8,2,128,128]{3,2,1,0:T(8,128)}), (f32[8,128,128]{1,2,0:T(8,128)}, f32[8,2,128,128]{3,2,1,0:T(8,128)})) %all-reduce.16.cloned.1.call-update) | async-done | bytes 1572880 | tf_op jit(solution)/shard_map/psum | solution.py:53
  117.9 93.8 %custom-call.14 = f32[8,128,128]{2,1,0:T(8,128)S(1)} custom-call(f32[8,128,128]{2,1,0:T(8,128)S(1)} %fusion.31), custom_call_target="Cholesky" | custom-call | tf_op jit(solution)/shard_map/jit(cholesky)/cholesky | solution.py:19
  212.0 78.6 %custom-call.15 = f32[8,1,128,128]{2,3,1,0:T(8,128)S(1)} custom-call(f32[8,1,128,128]{3,2,1,0:T(8,128)S(1)} %select_bitcast_fusion.3), custom_call_target="InvertDiagBlocksLowerTriangular" | custom-call | tf_op jit(solution)/shard_map/vmap(jit(_cho_solve))/triangular_solve | solution.py:20
  296.4 15.1 %all-gather.1 = f32[32,128,32]{1,2,0:T(8,128)S(1)} all-gather(f32[8,128,32]{1,2,0:T(8,128)S(1)} %convolution_bitcast_fusion.6), channel_id=3, replica_groups=mesh['mem'=8,'st'=4] {'st'}, dimensions={0}, use_global_device_ids=true | all-gather | bytes 655360 | tf_op jit(solution)/shard_map/all_gather | solution.py:12
  311.6 12.2 %psum.101 = f32[8,128]{1,0:T(8,128)S(1)} all-reduce(f32[8,128]{1,0:T(8,128)S(1)} %bitcast_reduce_fusion.2), channel_id=1, replica_groups=mesh['mem'=8,'st'=4] {'mem'}, use_global_device_ids=true, to_apply=%region_9.12 | all-reduce | flops 1024 | bytes 8192 | tf_op jit(solution)/shard_map/psum | solution.py:51
  325.6 3.0 fusion.47
  328.9 58.7 %all-reduce.14.cloned.1.call-done = (f32[8,128,128]{1,2,0:T(8,128)}, f32[8,2,128,128]{3,2,1,0:T(8,128)}) async-done(((f32[8,128,128]{1,2,0:T(8,128)}, f32[8,2,128,128]{3,2,1,0:T(8,128)}), (f32[8,128,128]{1,2,0:T(8,128)}, f32[8,2,128,128]{3,2,1,0:T(8,128)})) %all-reduce.14.cloned.1.call-update) | async-done | bytes 1572880 | tf_op jit(solution)/shard_map/psum | solution.py:53
  390.1 93.8 %custom-call.16 = f32[8,128,128]{2,1,0:T(8,128)S(1)} custom-call(f32[8,128,128]{2,1,0:T(8,128)S(1)} %fusion.27), custom_call_target="Cholesky" | custom-call | tf_op jit(solution)/shard_map/jit(cholesky)/cholesky | solution.py:19
  484.1 78.6 %custom-call.17 = f32[8,1,128,128]{2,3,1,0:T(8,128)S(1)} custom-call(f32[8,1,128,128]{3,2,1,0:T(8,128)S(1)} %select_bitcast_fusion.2), custom_call_target="InvertDiagBlocksLowerTriangular" | custom-call | tf_op jit(solution)/shard_map/vmap(jit(_cho_solve))/triangular_solve | solution.py:20
  568.6 15.1 %all-gather.2 = f32[32,128,32]{1,2,0:T(8,128)S(1)} all-gather(f32[8,128,32]{1,2,0:T(8,128)S(1)} %convolution_bitcast_fusion.5), channel_id=4, replica_groups=mesh['mem'=8,'st'=4] {'st'}, dimensions={0}, use_global_device_ids=true | all-gather | bytes 655360 | tf_op jit(solution)/shard_map/all_gather | solution.py:12
  583.8 12.0 %psum.104 = f32[8,128]{1,0:T(8,128)S(1)} all-reduce(f32[8,128]{1,0:T(8,128)S(1)} %bitcast_reduce_fusion.1), channel_id=1, replica_groups=mesh['mem'=8,'st'=4] {'mem'}, use_global_device_ids=true, to_apply=%region_14.17 | all-reduce | flops 1024 | bytes 8192 | tf_op jit(solution)/shard_map/psum | solution.py:51
  597.6 3.0 fusion.44
  601.2 58.4 %all-reduce.12.cloned.1.call-done = (f32[8,128,128]{1,2,0:T(8,128)}, f32[8,2,128,128]{3,2,1,0:T(8,128)}) async-done(((f32[8,128,128]{1,2,0:T(8,128)}, f32[8,2,128,128]{3,2,1,0:T(8,128)}), (f32[8,128,128]{1,2,0:T(8,128)}, f32[8,2,128,128]{3,2,1,0:T(8,128)})) %all-reduce.12.cloned.1.call-update) | async-done | bytes 1572880 | tf_op jit(solution)/shard_map/psum | solution.py:53
  662.1 93.8 %custom-call.18 = f32[8,128,128]{2,1,0:T(8,128)S(1)} custom-call(f32[8,128,128]{2,1,0:T(8,128)S(1)} %fusion.23), custom_call_target="Cholesky" | custom-call | tf_op jit(solution)/shard_map/jit(cholesky)/cholesky | solution.py:19
  756.2 78.6 %custom-call.19 = f32[8,1,128,128]{2,3,1,0:T(8,128)S(1)} custom-call(f32[8,1,128,128]{3,2,1,0:T(8,128)S(1)} %select_bitcast_fusion.1), custom_call_target="InvertDiagBlocksLowerTriangular" | custom-call | tf_op jit(solution)/shard_map/vmap(jit(_cho_solve))/triangular_solve | solution.py:20
  840.7 15.1 %all-gather.3 = f32[32,128,32]{1,2,0:T(8,128)S(1)} all-gather(f32[8,128,32]{1,2,0:T(8,128)S(1)} %convolution_bitcast_fusion.4), channel_id=5, replica_groups=mesh['mem'=8,'st'=4] {'st'}, dimensions={0}, use_global_device_ids=true | all-gather | bytes 655360 | tf_op jit(solution)/shard_map/all_gather | solution.py:12
  856.6 12.4 %pmax.7 = f32[]{:T(128)} all-reduce(f32[]{:T(128)} %get-tuple-element.20), channel_id=1, replica_groups=mesh['mem'=8,'st'=4] {'mem'}, use_global_device_ids=true, to_apply=%region_27.30 | all-reduce | flops 1 | bytes 8 | tf_op jit(solution)/shard_map/pmax | solution.py:68
  870.3 12.9 %all-reduce = (f32[8,128]{1,0:T(8,128)S(1)}, f32[]{:T(128)}, f32[]{:T(128)}) all-reduce(f32[8,128]{1,0:T(8,128)S(1)} %bitcast_reduce_fusion, f32[]{:T(128)} %get-tuple-element.6, f32[]{:T(128)} %get-tuple-element.5), channel_id=1, replica_groups=mesh['mem'=8,'st'=4] {'mem'}, use_global_device_ids=true, to_apply=%region_19.22 | all-reduce | flops 1026 | bytes 8208 | tf_op jit(solution)/shard_map/psum | solution.py:51
  891.9 55.1 %all-reduce.10.cloned.1.call-done = (f32[8,128,128]{1,2,0:T(8,128)}, f32[8,2,128,128]{3,2,1,0:T(8,128)}) async-done(((f32[8,128,128]{1,2,0:T(8,128)}, f32[8,2,128,128]{3,2,1,0:T(8,128)}), (f32[8,128,128]{1,2,0:T(8,128)}, f32[8,2,128,128]{3,2,1,0:T(8,128)})) %all-reduce.10.cloned.1.call-update) | async-done | bytes 1572880 | tf_op jit(solution)/shard_map/psum | solution.py:53
  949.5 93.8 %custom-call.20 = f32[8,128,128]{2,1,0:T(8,128)S(1)} custom-call(f32[8,128,128]{2,1,0:T(8,128)S(1)} %fusion.19), custom_call_target="Cholesky" | custom-call | tf_op jit(solution)/shard_map/jit(cholesky)/cholesky | solution.py:19
  1043.6 78.6 %custom-call.21 = f32[8,1,128,128]{2,3,1,0:T(8,128)S(1)} custom-call(f32[8,1,128,128]{3,2,1,0:T(8,128)S(1)} %select_bitcast_fusion), custom_call_target="InvertDiagBlocksLowerTriangular" | custom-call | tf_op jit(solution)/shard_map/vmap(jit(_cho_solve))/triangular_solve | solution.py:20
  (113 shorter events, 53.9 us)
Async XLA Ops:
  7.2 43.6 %copy-start.4 = (f32[4,8,128]{2,1,0:T(8,128)S(1)}, f32[4,8,128]{2,1,0:T(8,128)}, u32[]{:S(2)}) copy-start(f32[4,8,128]{2,1,0:T(8,128)} %param.10) | copy-start | bytes 49156
  7.2 49.1 %copy-start.5 = (f32[4,8,128]{2,1,0:T(8,128)S(1)}, f32[4,8,128]{2,1,0:T(8,128)}, u32[]{:S(2)}) copy-start(f32[4,8,128]{2,1,0:T(8,128)} %param.11) | copy-start | bytes 49156
  7.2 108.2 %all-reduce.16.cloned.1.call-start = ((), (), s32[]{:S(2)}) async-start(), calls=%async_computation.3 | async-start | bytes 3145728 | tf_op jit(solution)/shard_map/psum | solution.py:53
  55.7 331.9 %all-reduce.14.cloned.1.call-start = ((), (), s32[]{:S(2)}) async-start(), calls=%async_computation.2 | async-start | bytes 3145728 | tf_op jit(solution)/shard_map/psum | solution.py:53
  115.3 176.7 %copy-start = (f32[8,2,128,128]{3,2,1,0:T(8,128)S(1)}, f32[8,2,128,128]{3,2,1,0:T(8,128)}, u32[]{:S(2)}) copy-start(f32[8,2,128,128]{3,2,1,0:T(8,128)} %get-tuple-element.17) | copy-start | bytes 3145732
  328.6 331.0 %all-reduce.12.cloned.1.call-start = ((), (), s32[]{:S(2)}) async-start(), calls=%async_computation.1 | async-start | bytes 3145728 | tf_op jit(solution)/shard_map/psum | solution.py:53
  387.5 176.7 %copy-start.3 = (f32[8,2,128,128]{3,2,1,0:T(8,128)S(1)}, f32[8,2,128,128]{3,2,1,0:T(8,128)}, u32[]{:S(2)}) copy-start(f32[8,2,128,128]{3,2,1,0:T(8,128)} %get-tuple-element.15) | copy-start | bytes 3145732
  600.6 346.4 %all-reduce.10.cloned.1.call-start = ((), (), s32[]{:S(2)}) async-start(), calls=%async_computation | async-start | bytes 3145728 | tf_op jit(solution)/shard_map/psum | solution.py:53
  659.6 176.7 %copy-start.1 = (f32[8,2,128,128]{3,2,1,0:T(8,128)S(1)}, f32[8,2,128,128]{3,2,1,0:T(8,128)}, u32[]{:S(2)}) copy-start(f32[8,2,128,128]{3,2,1,0:T(8,128)} %get-tuple-element.13) | copy-start | bytes 3145732
  947.0 176.7 %copy-start.2 = (f32[8,2,128,128]{3,2,1,0:T(8,128)S(1)}, f32[8,2,128,128]{3,2,1,0:T(8,128)}, u32[]{:S(2)}) copy-start(f32[8,2,128,128]{3,2,1,0:T(8,128)} %get-tuple-element.11) | copy-start | bytes 3145732
Sparse Core Ops, SparseCore 0:
  55.8 59.5 all-reduce.15
  328.8 58.7 all-reduce.13
  600.7 58.8 all-reduce.11
  888.2 58.7 all-reduce.9
